TPU v7x, 32 devices: a whole 2x2x4 slice. The times are simulated.
32 devices in a mesh: group: 1, expert: 16 (over z, y, x), dp: 2 (over core).
Axes of the slice: x: 2, y: 2, z: 4, core: 2. Of those that a mesh axis runs over, the one named last changes fastest.
Arguments:
- tokens: bfloat16 [2048, 4096], P(('group', 'expert', 'dp')), may hold values from -6 to 6
- queries: bfloat16 [2048, 4096], P(('group', 'expert', 'dp')), may hold values from -6 to 6
- keys_local: bfloat16 [2048, 256], P(('group', 'expert', 'dp')), may hold values from -6 to 6
- values_local: bfloat16 [2048, 256], P(('group', 'expert', 'dp')), may hold values from -6 to 6
- prompt_keys: bfloat16 [1024, 256], P('group'), may hold values from -6 to 6
- prompt_values: bfloat16 [1024, 256], P('group'), may hold values from -6 to 6
- norm_gain: float32 [4096], replicated, may hold values from 0.25 to 1.75
- expert_ids: int32 [2048, 8], P(('group', 'expert', 'dp')), may hold values from 0 to 15, all different within a row; in each aligned block of 64 rows (0 to 63, 64 to 127, ...) at most 42 rows name the same one
- route_weight: float32 [2048, 8], P(('group', 'expert', 'dp')), may hold values from 0.05 to 1
- stored_gate: bfloat16 [16, 4096, 768], P('expert', None, 'dp'), may hold values from -0.09375 to 0.09375
- stored_up: bfloat16 [16, 4096, 768], P('expert', None, 'dp'), may hold values from -0.09375 to 0.09375
- stored_down: bfloat16 [16, 768, 4096], P('expert', 'dp'), may hold values from -0.21875 to 0.21875
- holder: int32 [16], replicated, may hold values from 0 to 15, as said below
Outputs:
- layer_out: bfloat16 [2048, 4096], P(('group', 'expert', 'dp'))
Inputs may be any that keep to these rules, and one draw needn't show every extreme that they name: `expert_ids`: each row names 8 different experts. In the 64 rows of one device no expert is named more than 42 times, and in every draw some expert is named exactly 42 times in some device's rows. holder[s] is s or the slot 8 away (s + 16 / 2 modulo 16), holder[holder[s]] = s, and holder[0] = 8.
All inputs are finite; a program needn't handle non-finite values.
Results may differ from a plain program's by a relative error of at most 0.0055.
Values may be sent and summed in bfloat16 or wider, within the bound.
A program may use at most 192 MiB of HBM per device.

v0:
```python
import jax
import jax.numpy as jnp
from jax import lax
from jax.experimental import pallas as pl
from jax.experimental.pallas import tpu as pltpu
from jax.sharding import PartitionSpec as P

HEADS = 32
KVH = 2
HD = 128
TOPK = 8
EXP_DEV = 1
PREFIX = 1024


def attend_rows(queries, keys_local, values_local, prompt_keys, prompt_values):
    count_rows = queries.shape[0]
    grouping = HEADS // KVH
    query_all = queries.reshape(count_rows, KVH, grouping, HD)
    key_all = jnp.concatenate([prompt_keys, keys_local], 0).reshape(-1, KVH, HD)
    value_all = jnp.concatenate([prompt_values, values_local], 0).reshape(-1, KVH, HD)
    scores = jnp.einsum(
        "tkgd,skd->kgts", query_all, key_all, preferred_element_type=jnp.float32
    ) * HD ** (-0.5)
    column = jnp.arange(key_all.shape[0], dtype=jnp.int32)
    row_index = jnp.arange(count_rows, dtype=jnp.int32)
    allowed = (column[None, :] < PREFIX) | (column[None, :] - PREFIX <= row_index[:, None])
    scores = jnp.where(allowed[None, None], scores, -jnp.inf)
    highest = jnp.max(scores, axis=-1, keepdims=True)
    expons = jnp.exp(scores - highest)
    weights = (expons / jnp.sum(expons, axis=-1, keepdims=True)).astype(jnp.bfloat16)
    context = jnp.einsum("kgts,skd->tkgd", weights, value_all, preferred_element_type=jnp.float32)
    return context.reshape(count_rows, HEADS * HD)


def expert_rows(picked, gate_w, up_w, down_w):
    gate_val = jnp.dot(picked, gate_w, preferred_element_type=jnp.float32)
    up_val = jnp.dot(picked, up_w, preferred_element_type=jnp.float32)
    hidden = (jax.nn.silu(gate_val) * up_val).astype(jnp.bfloat16)
    return jnp.dot(hidden, down_w, preferred_element_type=jnp.float32).astype(jnp.bfloat16)


def ffn_body(x_ref, w_ref, gate_ref, up_ref, down_ref, out_ref):
    rows = x_ref[...]
    gate_val = jnp.dot(rows, gate_ref[0], preferred_element_type=jnp.float32)
    up_val = jnp.dot(rows, up_ref[0], preferred_element_type=jnp.float32)
    hidden = gate_val / (1.0 + jnp.exp(-gate_val)) * up_val * w_ref[...]
    out_ref[...] = jnp.dot(
        hidden.astype(jnp.bfloat16), down_ref[0], preferred_element_type=jnp.float32
    ).astype(jnp.bfloat16)


def dense_ffn(rows, scale, gate_w, up_w, down_w):
    count, width = rows.shape[0], gate_w.shape[1]
    tile = 256
    return pl.pallas_call(
        ffn_body,
        grid=(count // tile,),
        out_shape=jax.ShapeDtypeStruct((count, width), jnp.bfloat16),
        in_specs=[
            pl.BlockSpec((tile, width), lambda i: (i, 0)),
            pl.BlockSpec((tile, 1), lambda i: (i, 0)),
            pl.BlockSpec(gate_w.shape, lambda i: (0, 0, 0), pipeline_mode=pl.Buffered(1)),
            pl.BlockSpec(up_w.shape, lambda i: (0, 0, 0), pipeline_mode=pl.Buffered(1)),
            pl.BlockSpec(down_w.shape, lambda i: (0, 0, 0), pipeline_mode=pl.Buffered(1)),
        ],
        out_specs=pl.BlockSpec((tile, width), lambda i: (i, 0)),
        compiler_params=pltpu.CompilerParams(
            dimension_semantics=("arbitrary",), vmem_limit_bytes=48 * 1024 * 1024
        ),
    )(rows, scale, gate_w, up_w, down_w)


def dense_mixture(normed, shares, expert_ids, gate_w, up_w, down_w, holder):
    owners = lax.axis_size("expert")
    axes = ("expert", "dp")
    named = expert_ids[:, :, None] == jnp.arange(owners, dtype=jnp.int32)[None, None, :]
    table = jnp.sum(jnp.where(named, shares[:, :, None], 0.0), axis=1)
    high = table.astype(jnp.bfloat16)
    low = (table - high.astype(jnp.float32)).astype(jnp.bfloat16)
    spread = lax.all_gather(jnp.concatenate([high, low], axis=1), axes, axis=0, tiled=True)
    rows = lax.all_gather(normed, axes, axis=0, tiled=True)
    mine = holder[lax.axis_index("expert")]
    pick = jnp.arange(2 * owners, dtype=jnp.int32) % owners == mine
    scale = jnp.sum(jnp.where(pick[None], spread.astype(jnp.float32), 0.0), axis=1, keepdims=True)
    partial_out = dense_ffn(rows, scale, gate_w, up_w, down_w)
    return lax.psum_scatter(partial_out, axes, scatter_dimension=0, tiled=True).astype(jnp.float32)


def local(
    tokens,
    queries,
    keys_local,
    values_local,
    prompt_keys,
    prompt_values,
    norm_gain,
    expert_ids,
    route_weight,
    stored_gate,
    stored_up,
    stored_down,
    holder,
):
    owners = lax.axis_size("expert")
    tok_count = tokens.shape[0]
    model_width = tokens.shape[1]
    capacity = min(tok_count, max(2, tok_count * TOPK * 4 // (3 * owners * EXP_DEV)))
    gate_w = stored_gate[0]
    up_w = stored_up[0]
    down_w = stored_down[0]
    context = attend_rows(queries, keys_local, values_local, prompt_keys, prompt_values)
    widened = tokens.astype(jnp.float32)
    normed = (
        widened * lax.rsqrt(jnp.mean(widened * widened, axis=-1, keepdims=True) + 1e-06) * norm_gain
    ).astype(jnp.bfloat16)
    shares = route_weight / jnp.sum(route_weight, axis=-1, keepdims=True)
    devices = owners * lax.axis_size("dp")
    if devices * tok_count <= 2 * lax.axis_size("dp") * owners * capacity:
        mixture = dense_mixture(
            normed, shares, expert_ids, stored_gate, stored_up, stored_down, holder
        )
        return (widened + context + mixture).astype(jnp.bfloat16)
    flat_ids = expert_ids.reshape(-1)
    onehot = (flat_ids[:, None] == jnp.arange(owners, dtype=jnp.int32)[None, :]).astype(jnp.int32)
    earlier = jnp.cumsum(onehot, axis=0) - onehot
    slot_of = jnp.sum(earlier * onehot, axis=1)
    places = (holder[flat_ids] * capacity + slot_of).reshape(tok_count, TOPK)
    chooser = (
        (jnp.arange(owners * capacity, dtype=jnp.int32)[:, None, None] == places[None])
        .any(axis=2)
        .astype(jnp.bfloat16)
    )
    send_rows = (
        jnp.dot(chooser, normed, preferred_element_type=jnp.float32)
        .astype(jnp.bfloat16)
        .reshape(owners, capacity, model_width)
    )
    both_rows = lax.all_gather(
        lax.all_to_all(send_rows, "expert", split_axis=0, concat_axis=0, tiled=True)[None],
        "dp",
        axis=0,
        tiled=True,
    )
    partial_out = expert_rows(both_rows.reshape(-1, model_width), gate_w, up_w, down_w)
    partial_out = partial_out.astype(jnp.float32).reshape(both_rows.shape)
    own_sum = lax.psum_scatter(
        partial_out.astype(jnp.bfloat16), "dp", scatter_dimension=0, tiled=True
    ).astype(jnp.float32)[0]
    results = lax.all_to_all(
        own_sum.astype(jnp.bfloat16), "expert", split_axis=0, concat_axis=0, tiled=True
    )
    gathered = results.reshape(owners * capacity, model_width)[places]
    mixture = jnp.einsum("tk,tkd->td", shares, gathered.astype(jnp.float32))
    return (widened + context + mixture).astype(jnp.bfloat16)


def solution(mesh):
    return jax.shard_map(
        local,
        mesh=mesh,
        in_specs=(
            P(("group", "expert", "dp"), None),
            P(("group", "expert", "dp"), None),
            P(("group", "expert", "dp"), None),
            P(("group", "expert", "dp"), None),
            P("group", None),
            P("group", None),
            P(),
            P(("group", "expert", "dp"), None),
            P(("group", "expert", "dp"), None),
            P("expert", None, "dp"),
            P("expert", None, "dp"),
            P("expert", "dp", None),
            P(),
        ),
        out_specs=P(("group", "expert", "dp"), None),
        check_vma=False,
    )
```

profile of v0, /device:TPU:0, one launch (start us, length us, event | category | flops | bytes accessed | tf_op | source)
XLA Modules:
  0.0 353.7 jit_solution(7599875951745467530)
XLA Ops:
  6.5 0.0 all-gather.3.cloned.1.call-start
  6.5 1.2 fusion.11
  7.8 2.0 fusion.13
  9.8 0.0 all-gather.3.cloned.1.call-update
  9.9 0.0 reduce-scatter.2.cloned.1.call-start
  9.9 0.7 reduce_sum.47
  10.6 0.7 broadcast_divide_fusion
  11.3 0.7 select_reduce_fusion.1
  12.0 45.4 %all-gather = bf16[32,64,32]{1,2,0:T(8,128)(2,1)S(1)} all-gather(bf16[1,64,32]{1,2,0:T(8,128)(2,1)S(1)} %maximum_bitcast_fusion), channel_id=1, replica_groups=mesh['group'=1,'expert'=16,'dp'=2] {'expert','dp'}, dimensions={0}, use_global_device_ids=true | all-gather | bytes 135168 | tf_op jit(solution)/shard_map/all_gather | solution.py:81
  57.4 0.1 copy.52
  57.5 0.2 reshape.87
  57.7 1.2 dynamic_slice.3
  58.9 0.6 fusion.25
  59.5 0.1 select_reduce_fusion
  59.6 0.4 copy.53.w_ref
  60.0 68.1 %all-gather.3.cloned.1.call-done.x_ref = bf16[2048,4096]{1,0:T(8,128)(2,1)} async-done(((bf16[64,4096]{1,0:T(8,128)(2,1)}), bf16[2048,4096]{1,0:T(8,128)(2,1)}) %all-gather.3.cloned.1.call-update) | async-done | bytes 16777232 | tf_op jit(solution)/shard_map/all_gather | solution.py:82
  128.1 0.0 copy-start
  128.1 1.9 copy-done
  130.0 33.0 %shard_map.127 = bf16[2048,4096]{1,0:T(8,128)(2,1)} custom-call(bf16[2048,4096]{1,0:T(8,128)(2,1)} %all-gather.3.cloned.1.call-done.x_ref, f32[2048,1]{1,0:T(8,128)S(1)} %copy.53.w_ref, bf16[1,4096,384]{2,1,0:T(8,128)(2,1)S(1)} %copy-done, bf16[1,4096,384]{2,1,0:T(8,128)(2,1)} %up_ref.1, bf16[1,384,4096]{2,1,0:T(8,128)(2,1)} %down_ref.1), custom_call_target="tpu_custom_call" | custom-call | tf_op jit(solution)/shard_map/pallas_call | solution.py:56
  163.0 0.0 copy-start.2
  163.0 0.0 copy-start.5
  163.0 0.0 copy-start.3
  163.0 0.0 copy-start.4
  163.0 0.0 copy-start.6
  163.1 0.0 reduce-scatter.2.cloned.1.call-update
  163.1 1.0 copy-done.2
  164.1 0.0 copy-done.5
  164.1 0.3 copy.47
  164.4 0.0 copy-done.3
  164.4 0.1 copy.60
  164.5 0.0 copy-done.4
  164.5 0.0 copy-done.6
  164.6 0.3 copy.46
  164.9 0.1 fusion.20
  165.0 3.7 %fusion.32 = f32[2,16,64]{2,1,0:T(8,128)S(1)} fusion(pred[64,1088]{1,0:T(8,128)(4,1)S(1)} %fusion.20, bf16[1088,2,128,1]{0,2,3,1:T(8,128)(2,1)S(1)} %bitcast.40, bf16[64,2,16,128]{3,2,1,0:T(8,128)(2,1)S(1)} %bitcast.44), kind=kOutput, calls=%fused_computation.41 | convolution fusion | flops 579339328 | bytes 1159168 | tf_op jit(solution)/shard_map/sub | solution.py:30
  168.6 0.0 copy-start.1
  168.6 4.9 %fusion.6 = f32[64,2,16,128]{3,0,2,1:T(8,128)S(1)} fusion(bf16[1088,2,128,1]{0,2,3,1:T(8,128)(2,1)S(1)} %bitcast.42, f32[2,16,64]{2,1,0:T(8,128)S(1)} %fusion.32, pred[64,1088]{1,0:T(8,128)(4,1)S(1)} %fusion.20, bf16[1088,2,128,1]{0,2,3,1:T(8,128)(2,1)S(1)} %bitcast.41, bf16[64,2,16,128]{3,2,1,0:T(8,128)(2,1)S(1)} %bitcast.45), kind=kOutput, calls=%fused_computation.12 | convolution fusion | flops 1151994880 | bytes 2764800 | tf_op jit(solution)/shard_map/kgts,skd->tkgd/dot_general | solution.py:32
  173.5 0.6 copy.51
  174.1 170.3 %reduce-scatter.2.cloned.1.call-done = bf16[64,4096]{1,0:T(8,128)(2,1)} async-done(((bf16[2048,4096]{1,0:T(8,128)(2,1)}), bf16[64,4096]{1,0:T(8,128)(2,1)}) %reduce-scatter.2.cloned.1.call-update) | async-done | bytes 524304 | tf_op jit(solution)/shard_map/reduce_scatter | solution.py:87
  344.4 0.0 copy-done.1
  344.4 2.5 fusion.10
  (7 shorter events, 0.1 us)
Async XLA Ops:
  6.5 121.6 %all-gather.3.cloned.1.call-start = ((), (), s32[]{:S(2)}) async-start(), calls=%async_computation.1 | async-start | bytes 17301504 | tf_op jit(solution)/shard_map/all_gather | solution.py:82
  9.9 334.5 %reduce-scatter.2.cloned.1.call-start = ((), (), s32[]{:S(2)}) async-start(), calls=%async_computation.2 | async-start | bytes 17301504 | tf_op jit(solution)/shard_map/reduce_scatter | solution.py:87
  128.1 1.9 copy-start
  163.0 1.0 copy-start.2
  163.0 1.0 copy-start.5
  163.0 1.4 copy-start.3
  163.0 1.5 copy-start.4
  163.0 1.5 copy-start.6
  168.6 175.8 %copy-start.1 = (bf16[64,4096]{1,0:T(8,128)(2,1)S(1)}, bf16[64,4096]{1,0:T(8,128)(2,1)}, u32[]{:S(2)}) copy-start(bf16[64,4096]{1,0:T(8,128)(2,1)} %param.13) | copy-start | bytes 1572868
Sparse Core Ops, SparseCore 0:
  10.2 117.8 all-gather.2
  163.2 181.1 reduce-scatter.1
where the time goes:
time: 354 us
  waiting for transfers between devices  238 us (67%)
  blocking collectives  45.4 us (13%)
  Pallas kernels  33 us (9%)
  between operations  13.6 us (4%)
  other arithmetic  8.69 us (2%)
  matrix products  8.54 us (2%)
  local copies, waits for them, and re-layouts  6.06 us (2%)
    reduce_scatter x1, waiting for transfers between devices, dense_mixture(): lax.psum_scatter(partial_out, axes, scatter_dimension=0, tiled=True)  170 us
    all_gather x1, waiting for transfers between devices, dense_mixture(): rows = lax.all_gather(normed, axes, axis=0, tiled=True)  68.1 us
    all_gather x1, blocking collectives, dense_mixture(): lax.all_gather(jnp.concatenate([high, low], axis=1), axes, axis=0, tiled=...  45.4 us
    pallas_call x1, Pallas kernels, dense_ffn(): pl.pallas_call(ffn_body, grid=(count // tile,), out_shape=jax.ShapeDtypeS...  33 us
  transfers between devices with their start and end apart: 2, of which 2 were waited for; matrix products, arithmetic and copies ran while one was open for 4% of the time, Pallas kernels for 0%

commit v1 on v0

--- a/solution.py
+++ b/solution.py
@@ -1,3 +1,5 @@
+import functools
+
 import jax
 import jax.numpy as jnp
 from jax import lax
@@ -11,6 +13,8 @@
 TOPK = 8
 EXP_DEV = 1
 PREFIX = 1024
+PAIR = 2
+MESH = pl.DeviceIdType.MESH
 
 
 def attend_rows(queries, keys_local, values_local, prompt_keys, prompt_values):
@@ -40,51 +44,492 @@
     return jnp.dot(hidden, down_w, preferred_element_type=jnp.float32).astype(jnp.bfloat16)
 
 
-def ffn_body(x_ref, w_ref, gate_ref, up_ref, down_ref, out_ref):
-    rows = x_ref[...]
-    gate_val = jnp.dot(rows, gate_ref[0], preferred_element_type=jnp.float32)
-    up_val = jnp.dot(rows, up_ref[0], preferred_element_type=jnp.float32)
-    hidden = gate_val / (1.0 + jnp.exp(-gate_val)) * up_val * w_ref[...]
-    out_ref[...] = jnp.dot(
-        hidden.astype(jnp.bfloat16), down_ref[0], preferred_element_type=jnp.float32
-    ).astype(jnp.bfloat16)
-
-
-def dense_ffn(rows, scale, gate_w, up_w, down_w):
-    count, width = rows.shape[0], gate_w.shape[1]
-    tile = 256
+def rows_of(place, count):
+    return pl.ds(place * count, count)
+
+
+def layer_body(
+    slots,
+    chunks,
+    room,
+    tok_ref,
+    query_ref,
+    key_ref,
+    value_ref,
+    pkey_ref,
+    pvalue_ref,
+    gain_ref,
+    ids_ref,
+    weight_ref,
+    holder_ref,
+    gate_hbm,
+    up_hbm,
+    down_hbm,
+    out_ref,
+    line_own,
+    line_pair,
+    packed,
+    mine_rows,
+    leaf_rows,
+    mine_res,
+    leaf_res,
+    back_res,
+    pair_sum,
+    pair_got,
+    line_sum,
+    line_got,
+    proj_w,
+    down_w,
+    mine_acc,
+    leaf_acc,
+    mine_hid,
+    leaf_hid,
+    context,
+    table_own,
+    table_pair,
+    chooser,
+    spread,
+    line_send,
+    line_recv,
+    pair_send,
+    pair_recv,
+    leaf_send,
+    leaf_recv,
+    back_send,
+    back_recv,
+    sum_send,
+    sum_recv,
+    end_send,
+    end_recv,
+    table_send,
+    table_recv,
+    load_sem,
+    give_send,
+    give_recv,
+):
+    tok = tok_ref.shape[0]
+    span = tok_ref.shape[1] // chunks
+    unit = gate_hbm.shape[2]
+    full = slots * tok
+    plane = PAIR * PAIR
+    me, core = lax.axis_index("expert"), lax.axis_index("dp")
+    level, spot = me // plane, lax.rem(me, plane)
+    low = 1 - 2 * lax.rem(spot, PAIR)
+    high = PAIR - 2 * PAIR * (spot // PAIR)
+    pair_id = me + (1 - core) * low + core * high
+    leaf_id = me + core * low + (1 - core) * high
+    ahead = [lax.rem(level + k, slots) * plane + spot for k in range(slots)]
+    behind = [lax.rem(level + slots - k, slots) * plane + spot for k in range(slots)]
+
+    def remote(src, dst, send, recv, expert, side=core):
+        return pltpu.make_async_remote_copy(
+            src_ref=src,
+            dst_ref=dst,
+            send_sem=send,
+            recv_sem=recv,
+            device_id={"expert": expert, "dp": side},
+            device_id_type=MESH,
+        )
+
+    def line_copy(ch, k):
+        return remote(
+            line_own.at[ch, rows_of(0, tok)],
+            line_own.at[ch, rows_of(k, tok)],
+            line_send.at[ch, k - 1],
+            line_recv.at[ch, k - 1],
+            ahead[k],
+        )
+
+    def pair_copy(ch):
+        return remote(line_own.at[ch], line_pair.at[ch], pair_send.at[ch], pair_recv.at[ch], pair_id)
+
+    def leaf_copy(ch, g):
+        return remote(
+            packed.at[ch, rows_of(g, room)],
+            leaf_rows.at[ch, rows_of(g, room)],
+            leaf_send.at[ch, g],
+            leaf_recv.at[ch, g],
+            leaf_id,
+        )
+
+    def back_copy(ch, g):
+        return remote(
+            leaf_res.at[ch, rows_of(g, room)],
+            back_res.at[ch, rows_of(g, room)],
+            back_send.at[ch, g],
+            back_recv.at[ch, g],
+            leaf_id,
+        )
+
+    def sum_copy(ch):
+        return remote(pair_sum.at[ch], pair_got.at[ch], sum_send.at[ch], sum_recv.at[ch], pair_id)
+
+    def end_copy(ch, k):
+        return remote(
+            line_sum.at[ch, rows_of(k, tok)],
+            line_got.at[ch, rows_of(k - 1, tok)],
+            end_send.at[ch, k - 1],
+            end_recv.at[ch, k - 1],
+            behind[k],
+        )
+
+    def table_line(k):
+        return remote(
+            table_own.at[rows_of(0, tok)],
+            table_own.at[rows_of(k, tok)],
+            table_send.at[k],
+            table_recv.at[k],
+            ahead[k],
+        )
+
+    def table_across():
+        return remote(table_own, table_pair, table_send.at[0], table_recv.at[0], pair_id)
+
+    def weight_parts():
+        return (
+            (gate_hbm.at[0], lambda p: proj_w.at[:, pl.ds(p * unit, unit)]),
+            (up_hbm.at[0], lambda p: proj_w.at[:, pl.ds((2 + p) * unit, unit)]),
+            (down_hbm.at[0], lambda p: down_w.at[rows_of(p, unit)]),
+        )
+
+    def load(n):
+        src, dst = weight_parts()[n]
+        return pltpu.make_async_copy(src, dst(0), load_sem.at[n])
+
+    def give(n):
+        src, dst = weight_parts()[n]
+        return remote(src, dst(1), give_send.at[n], give_recv.at[n], me, 1 - core)
+
+    for n in range(3):
+        load(n).start()
+
+    barrier = pltpu.get_barrier_semaphore()
+    for k in range(1, slots):
+        pl.semaphore_signal(barrier, inc=1, device_id={"expert": ahead[k], "dp": core}, device_id_type=MESH)
+    for expert, side in ((pair_id, core), (leaf_id, core), (me, 1 - core)):
+        pl.semaphore_signal(barrier, inc=1, device_id={"expert": expert, "dp": side}, device_id_type=MESH)
+
+    lanes = lax.broadcasted_iota(jnp.int32, table_pair.shape[:0] + (tok, table_pair.shape[1]), 1)
+    raw = weight_ref[...]
+    share = raw / jnp.sum(raw, axis=-1, keepdims=True)
+    named = ids_ref[...]
+    entry = jnp.zeros(lanes.shape, jnp.float32)
+    for k in range(TOPK):
+        entry = entry + jnp.where(lanes == named[:, k : k + 1], share[:, k : k + 1], 0.0)
+    table_own[pl.ds(0, tok), :] = entry.astype(jnp.bfloat16)
+
+    widened = tok_ref[...].astype(jnp.float32)
+    inverse = lax.rsqrt(jnp.mean(widened * widened, axis=-1, keepdims=True) + 1e-06)
+    for ch in range(chunks):
+        cols = pl.ds(ch * span, span)
+        line_own[ch, pl.ds(0, tok), :] = (
+            tok_ref[:, cols].astype(jnp.float32) * inverse * gain_ref[:, cols]
+        ).astype(jnp.bfloat16)
+
+    pl.semaphore_wait(barrier, slots - 1 + 3)
+
+    for k in range(1, slots):
+        table_line(k).start()
+
+    def send_line(ch, carry):
+        for k in range(1, slots):
+            line_copy(ch, k).start()
+        return carry
+
+    lax.fori_loop(0, chunks, send_line, 0)
+    for n in range(3):
+        give(n).start()
+
+    def choose(table, expert, place):
+        sel = (
+            lax.broadcasted_iota(jnp.int32, (table.shape[1], full), 0) == expert
+        ).astype(jnp.float32).astype(jnp.bfloat16)
+        portion = jnp.dot(table[...], sel, preferred_element_type=jnp.float32)
+        taken = portion > 0.0
+        row = lax.broadcasted_iota(jnp.int32, (full, full), 0)
+        col = lax.broadcasted_iota(jnp.int32, (full, full), 1)
+        before = (col < row).astype(jnp.float32).astype(jnp.bfloat16)
+        rank = jnp.dot(
+            before, taken.astype(jnp.float32).astype(jnp.bfloat16), preferred_element_type=jnp.float32
+        )
+        hit = taken & (rank == col.astype(jnp.float32))
+        spread[place] = jnp.where(hit, portion, 0.0)[:, :room].astype(jnp.bfloat16)
+        chooser[place] = jnp.where(hit, 1.0, 0.0).T[:room].astype(jnp.bfloat16)
+
+    my_expert, leaf_expert = holder_ref[me], holder_ref[leaf_id]
+
+    for k in range(1, slots):
+        table_line(k).wait_recv()
+    table_across().start()
+    choose(table_own, leaf_expert, 1)
+    choose(table_own, my_expert, 0)
+
+    group = HEADS // KVH
+    heads = span // HD
+    late = (
+        lax.broadcasted_iota(jnp.int32, (heads * tok, tok), 1)
+        > lax.rem(lax.broadcasted_iota(jnp.int32, (heads * tok, tok), 0), tok)
+    )
+
+    def attend(ch):
+        asked = jnp.concatenate(
+            [query_ref[:, pl.ds(pl.multiple_of(ch * span + h * HD, HD), HD)] for h in range(heads)], axis=0
+        )
+        cols = pl.ds(pl.multiple_of((ch * heads) // group * HD, HD), HD)
+        over = (((1,), (1,)), ((), ()))
+        first = lax.dot_general(asked, pkey_ref[:, cols], over, preferred_element_type=jnp.float32)
+        second = lax.dot_general(asked, key_ref[:, cols], over, preferred_element_type=jnp.float32)
+        first = first * HD ** (-0.5)
+        second = jnp.where(late, -jnp.inf, second * HD ** (-0.5))
+        peak = jnp.maximum(
+            jnp.max(first, axis=-1, keepdims=True), jnp.max(second, axis=-1, keepdims=True)
+        )
+        first, second = jnp.exp(first - peak), jnp.exp(second - peak)
+        total = jnp.sum(first, axis=-1, keepdims=True) + jnp.sum(second, axis=-1, keepdims=True)
+        scale = 1.0 / total
+        found = jnp.dot(
+            (first * scale).astype(jnp.bfloat16), pvalue_ref[:, cols], preferred_element_type=jnp.float32
+        ) + jnp.dot(
+            (second * scale).astype(jnp.bfloat16), value_ref[:, cols], preferred_element_type=jnp.float32
+        )
+        for h in range(heads):
+            context[ch, :, pl.ds(h * HD, HD)] = found[h * tok : (h + 1) * tok]
+
+    def pick(place, rows):
+        return jnp.dot(chooser[place], rows, preferred_element_type=jnp.float32).astype(jnp.bfloat16)
+
+    def project(acc, rows, ch):
+        part = jnp.dot(
+            rows, proj_w[pl.ds(pl.multiple_of(ch * span, span), span), :], preferred_element_type=jnp.float32
+        )
+
+        @pl.when(ch == 0)
+        def _():
+            acc[...] = part
+
+        @pl.when(ch > 0)
+        def _():
+            acc[...] += part
+
+    def activate(acc, hid):
+        gate = acc[:, : 2 * unit]
+        hid[...] = (gate / (1.0 + jnp.exp(-gate)) * acc[:, 2 * unit :]).astype(jnp.bfloat16)
+
+    def gather(i, carry):
+        @pl.when(i < chunks)
+        def _():
+            for k in range(1, slots):
+                line_copy(i, k).wait_recv()
+            pair_copy(i).start()
+            packed[i, pl.ds(0, room), :] = pick(1, line_own[i])
+            mine_rows[i, pl.ds(0, room), :] = pick(0, line_own[i])
+            leaf_copy(i, 0).start()
+            attend(i)
+
+        @pl.when(i == 1)
+        def _():
+            table_across().wait_recv()
+            choose(table_pair, leaf_expert, 3)
+            choose(table_pair, my_expert, 2)
+            for n in range(3):
+                load(n).wait()
+                give(n).wait_recv()
+
+        @pl.when((i >= 1) & (i <= chunks))
+        def _():
+            j = i - 1
+            pair_copy(j).wait_recv()
+            packed[j, pl.ds(room, room), :] = pick(3, line_pair[j])
+            mine_rows[j, pl.ds(room, room), :] = pick(2, line_pair[j])
+            leaf_copy(j, 1).start()
+            project(mine_acc, mine_rows[j], j)
+
+        @pl.when(i == chunks + 1)
+        def _():
+            activate(mine_acc, mine_hid)
+
+        @pl.when(i >= 2)
+        def _():
+            j = i - 2
+            for g in range(2):
+                leaf_copy(j, g).wait_recv()
+            project(leaf_acc, leaf_rows[j], j)
+
+        return carry
+
+    lax.fori_loop(0, chunks + 2, gather, 0)
+    activate(leaf_acc, leaf_hid)
+
+    def shrink(hid, ch):
+        return jnp.dot(
+            hid[...],
+            down_w[:, pl.ds(pl.multiple_of(ch * span, span), span)],
+            preferred_element_type=jnp.float32,
+        ).astype(jnp.bfloat16)
+
+    def leaf_down(ch, carry):
+        leaf_res[ch] = shrink(leaf_hid, ch)
+        back_copy(ch, 1).start()
+        back_copy(ch, 0).start()
+        return carry
+
+    def mine_down(ch, carry):
+        mine_res[ch] = shrink(mine_hid, ch)
+        return carry
+
+    lax.fori_loop(0, chunks, leaf_down, 0)
+    lax.fori_loop(0, chunks, mine_down, 0)
+
+    def merged(ch, g):
+        rows = pl.ds(g * room, room)
+        return jnp.dot(
+            spread[2 * g], mine_res[ch, rows, :], preferred_element_type=jnp.float32
+        ) + jnp.dot(spread[2 * g + 1], back_res[ch, rows, :], preferred_element_type=jnp.float32)
+
+    def reduce(i, carry):
+        @pl.when(i < chunks)
+        def _():
+            back_copy(i, 1).wait_recv()
+            pair_sum[i] = merged(i, 1).astype(jnp.bfloat16)
+            sum_copy(i).start()
+
+        @pl.when((i >= 1) & (i <= chunks))
+        def _():
+            j = i - 1
+            back_copy(j, 0).wait_recv()
+            half = merged(j, 0)
+            sum_copy(j).wait_recv()
+            line_sum[j] = (half + pair_got[j].astype(jnp.float32)).astype(jnp.bfloat16)
+            for k in range(1, slots):
+                end_copy(j, k).start()
+
+        @pl.when(i >= 2)
+        def _():
+            j = i - 2
+            cols = pl.ds(pl.multiple_of(j * span, span), span)
+            total = tok_ref[:, cols].astype(jnp.float32) + context[j]
+            mixture = line_sum[j, pl.ds(0, tok), :].astype(jnp.float32)
+            for k in range(1, slots):
+                end_copy(j, k).wait_recv()
+                mixture = mixture + line_got[j, rows_of(k - 1, tok), :].astype(jnp.float32)
+            out_ref[:, cols] = (total + mixture).astype(jnp.bfloat16)
+
+        return carry
+
+    lax.fori_loop(0, chunks + 2, reduce, 0)
+
+    def finish(ch, carry):
+        for k in range(1, slots):
+            line_copy(ch, k).wait_send()
+            end_copy(ch, k).wait_send()
+        for g in range(2):
+            leaf_copy(ch, g).wait_send()
+            back_copy(ch, g).wait_send()
+        pair_copy(ch).wait_send()
+        sum_copy(ch).wait_send()
+        return carry
+
+    lax.fori_loop(0, chunks, finish, 0)
+    table_across().wait_send()
+    for k in range(1, slots):
+        table_line(k).wait_send()
+    for n in range(3):
+        give(n).wait_send()
+
+
+def fused_layer(
+    capacity,
+    tokens,
+    queries,
+    keys_local,
+    values_local,
+    prompt_keys,
+    prompt_values,
+    norm_gain,
+    expert_ids,
+    route_weight,
+    stored_gate,
+    stored_up,
+    stored_down,
+    holder,
+):
+    tok, width = tokens.shape
+    owners = lax.axis_size("expert")
+    slots = owners // (PAIR * PAIR)
+    unit = stored_gate.shape[2]
+    chunks = 8
+    span = width // chunks
+    full = slots * tok
+    room = -(-slots * capacity // 16) * 16
+    bf16, f32 = jnp.bfloat16, jnp.float32
+    lanes = -(-owners // 128) * 128
+    vmem, hbm = pl.BlockSpec(memory_space=pltpu.VMEM), pl.BlockSpec(memory_space=pl.ANY)
+    dma = pltpu.SemaphoreType.DMA
     return pl.pallas_call(
-        ffn_body,
-        grid=(count // tile,),
-        out_shape=jax.ShapeDtypeStruct((count, width), jnp.bfloat16),
-        in_specs=[
-            pl.BlockSpec((tile, width), lambda i: (i, 0)),
-            pl.BlockSpec((tile, 1), lambda i: (i, 0)),
-            pl.BlockSpec(gate_w.shape, lambda i: (0, 0, 0), pipeline_mode=pl.Buffered(1)),
-            pl.BlockSpec(up_w.shape, lambda i: (0, 0, 0), pipeline_mode=pl.Buffered(1)),
-            pl.BlockSpec(down_w.shape, lambda i: (0, 0, 0), pipeline_mode=pl.Buffered(1)),
+        functools.partial(layer_body, slots, chunks, room),
+        out_shape=jax.ShapeDtypeStruct((tok, width), bf16),
+        in_specs=[vmem] * 9 + [pl.BlockSpec(memory_space=pltpu.SMEM)] + [hbm] * 3,
+        out_specs=vmem,
+        scratch_shapes=[
+            pltpu.VMEM((chunks, full, span), bf16),
+            pltpu.VMEM((chunks, full, span), bf16),
+            pltpu.VMEM((chunks, 2 * room, span), bf16),
+            pltpu.VMEM((chunks, 2 * room, span), bf16),
+            pltpu.VMEM((chunks, 2 * room, span), bf16),
+            pltpu.VMEM((chunks, 2 * room, span), bf16),
+            pltpu.VMEM((chunks, 2 * room, span), bf16),
+            pltpu.VMEM((chunks, 2 * room, span), bf16),
+            pltpu.VMEM((chunks, full, span), bf16),
+            pltpu.VMEM((chunks, full, span), bf16),
+            pltpu.VMEM((chunks, full, span), bf16),
+            pltpu.VMEM((chunks, (slots - 1) * tok, span), bf16),
+            pltpu.VMEM((width, 4 * unit), bf16),
+            pltpu.VMEM((2 * unit, width), bf16),
+            pltpu.VMEM((2 * room, 4 * unit), f32),
+            pltpu.VMEM((2 * room, 4 * unit), f32),
+            pltpu.VMEM((2 * room, 2 * unit), bf16),
+            pltpu.VMEM((2 * room, 2 * unit), bf16),
+            pltpu.VMEM((chunks, tok, span), f32),
+            pltpu.VMEM((full, lanes), bf16),
+            pltpu.VMEM((full, lanes), bf16),
+            pltpu.VMEM((4, room, full), bf16),
+            pltpu.VMEM((4, full, room), bf16),
+            dma((chunks, slots - 1)),
+            dma((chunks, slots - 1)),
+            dma((chunks,)),
+            dma((chunks,)),
+            dma((chunks, 2)),
+            dma((chunks, 2)),
+            dma((chunks, 2)),
+            dma((chunks, 2)),
+            dma((chunks,)),
+            dma((chunks,)),
+            dma((chunks, slots - 1)),
+            dma((chunks, slots - 1)),
+            dma((slots,)),
+            dma((slots,)),
+            dma((3,)),
+            dma((3,)),
+            dma((3,)),
         ],
-        out_specs=pl.BlockSpec((tile, width), lambda i: (i, 0)),
         compiler_params=pltpu.CompilerParams(
-            dimension_semantics=("arbitrary",), vmem_limit_bytes=48 * 1024 * 1024
+            collective_id=0, has_side_effects=True, vmem_limit_bytes=63 * 1024 * 1024
         ),
-    )(rows, scale, gate_w, up_w, down_w)
-
-
-def dense_mixture(normed, shares, expert_ids, gate_w, up_w, down_w, holder):
-    owners = lax.axis_size("expert")
-    axes = ("expert", "dp")
-    named = expert_ids[:, :, None] == jnp.arange(owners, dtype=jnp.int32)[None, None, :]
-    table = jnp.sum(jnp.where(named, shares[:, :, None], 0.0), axis=1)
-    high = table.astype(jnp.bfloat16)
-    low = (table - high.astype(jnp.float32)).astype(jnp.bfloat16)
-    spread = lax.all_gather(jnp.concatenate([high, low], axis=1), axes, axis=0, tiled=True)
-    rows = lax.all_gather(normed, axes, axis=0, tiled=True)
-    mine = holder[lax.axis_index("expert")]
-    pick = jnp.arange(2 * owners, dtype=jnp.int32) % owners == mine
-    scale = jnp.sum(jnp.where(pick[None], spread.astype(jnp.float32), 0.0), axis=1, keepdims=True)
-    partial_out = dense_ffn(rows, scale, gate_w, up_w, down_w)
-    return lax.psum_scatter(partial_out, axes, scatter_dimension=0, tiled=True).astype(jnp.float32)
+    )(
+        tokens,
+        queries,
+        keys_local,
+        values_local,
+        prompt_keys,
+        prompt_values,
+        norm_gain.reshape(1, width),
+        expert_ids,
+        route_weight,
+        holder,
+        stored_gate,
+        stored_up,
+        stored_down,
+    )
 
 
 def local(
@@ -109,18 +554,31 @@
     gate_w = stored_gate[0]
     up_w = stored_up[0]
     down_w = stored_down[0]
+    cores = lax.axis_size("dp")
+    devices = owners * cores
+    if devices * tok_count <= 2 * cores * owners * capacity and owners % (PAIR * PAIR) == 0 and cores == 2:
+        return fused_layer(
+            capacity,
+            tokens,
+            queries,
+            keys_local,
+            values_local,
+            prompt_keys,
+            prompt_values,
+            norm_gain,
+            expert_ids,
+            route_weight,
+            stored_gate,
+            stored_up,
+            stored_down,
+            holder,
+        )
     context = attend_rows(queries, keys_local, values_local, prompt_keys, prompt_values)
     widened = tokens.astype(jnp.float32)
     normed = (
         widened * lax.rsqrt(jnp.mean(widened * widened, axis=-1, keepdims=True) + 1e-06) * norm_gain
     ).astype(jnp.bfloat16)
     shares = route_weight / jnp.sum(route_weight, axis=-1, keepdims=True)
-    devices = owners * lax.axis_size("dp")
-    if devices * tok_count <= 2 * lax.axis_size("dp") * owners * capacity:
-        mixture = dense_mixture(
-            normed, shares, expert_ids, stored_gate, stored_up, stored_down, holder
-        )
-        return (widened + context + mixture).astype(jnp.bfloat16)
     flat_ids = expert_ids.reshape(-1)
     onehot = (flat_ids[:, None] == jnp.arange(owners, dtype=jnp.int32)[None, :]).astype(jnp.int32)
     earlier = jnp.cumsum(onehot, axis=0) - onehot

time: 354 us -> 157 us (0.44)
  waiting for transfers between devices: 238 us -> 0 us
  Pallas kernels: 33 us -> 152 us
  blocking collectives: 45.4 us -> 0 us
  between operations: 13.6 us -> 0.01 us
  other arithmetic: 8.69 us -> 0 us
  matrix products: 8.54 us -> 0 us
    reduce_scatter x1 -> x0, waiting for transfers between devices: 170 us -> none  [dense_mixture(): lax.psum_scatter(partial_out, axes, scatter_dimension=0, tiled=True)]
    pallas_call x1, Pallas kernels: 33 us -> 152 us  [fused_layer(): pl.pallas_call(functools.partial(layer_body, slots, chunks, room), out_sh...]
    all_gather x1 -> x0, waiting for transfers between devices: 68.1 us -> none  [dense_mixture(): rows = lax.all_gather(normed, axes, axis=0, tiled=True)]
    all_gather x1 -> x0, blocking collectives: 45.4 us -> none  [dense_mixture(): lax.all_gather(jnp.concatenate([high, low], axis=1), axes, axis=0, tiled=...]
    dot_general x1 -> x0, matrix products: 4.89 us -> none  [attend_rows(): jnp.einsum('kgts,skd->tkgd', weights, value_all, preferred_element_type=j...]
    convert_element_type x3 -> x0, other arithmetic: 4.53 us -> none  [the longest x1 2.49 us: local(): return (widened + context + mixture).astype(jnp.bfloat16)]
    sub x1 -> x0, matrix products: 3.65 us -> none  [attend_rows(): expons = jnp.exp(scores - highest)]
  transfers between devices with their start and end apart: 2 -> 0, of which waited for: 2 -> 0; matrix products, arithmetic and copies ran while one was open for 4% -> 0% of each run, Pallas kernels for 0% -> 0%
where the time goes in v1:
time: 157 us; the launch traced here: 156 us
  Pallas kernels  152 us (97%)
  local copies, waits for them, and re-layouts  4.62 us (3%)
    pallas_call x1, Pallas kernels, fused_layer(): pl.pallas_call(functools.partial(layer_body, slots, chunks, room), out_sh...  152 us
    unnamed x3, local copies, waits for them, and re-layouts  4.62 us

profile of v1, /device:TPU:0, one launch (start us, length us, event | category | flops | bytes accessed | tf_op | source)
XLA Modules:
  0.0 156.3 jit_solution(18216698802153541110)
XLA Ops:
  0.0 1.4 copy.14.ids_ref
  1.4 1.4 copy.15.weight_ref
  2.8 151.6 %shard_map.127 = bf16[64,4096]{1,0:T(8,128)(2,1)} custom-call(bf16[64,4096]{1,0:T(8,128)(2,1)} %tok_ref.1, bf16[64,4096]{1,0:T(8,128)(2,1)} %query_ref.1, bf16[64,256]{1,0:T(8,128)(2,1)} %key_ref.1, bf16[64,256]{1,0:T(8,128)(2,1)} %value_ref.1, bf16[1024,256]{1,0:T(8,128)(2,1)} %pkey_ref.1, bf16[1024,256]{1,0:T(8,128)(2,1)} %pvalue_ref.1, ...), custom_call_target="tpu_custom_call" | custom-call | tf_op jit(solution)/shard_map/pallas_call | solution.py:468
  154.4 1.9 %copy.17 = bf16[64,4096]{1,0:T(8,128)(2,1)} copy(bf16[64,4096]{1,0:T(8,128)(2,1)} %shard_map.127) | data formatting | bytes 1048576

commit v2 on v1

--- a/solution.py
+++ b/solution.py
@@ -89,7 +89,8 @@
     table_pair,
     chooser,
     spread,
-    line_send,
+    up_send,
+    down_send,
     line_recv,
     pair_send,
     pair_recv,
@@ -131,17 +132,24 @@
             device_id_type=MESH,
         )
 
-    def line_copy(ch, k):
+    def line_copy(ch, slot, send, expert):
+        part = line_own.at[ch, rows_of(slot, tok)]
+        return remote(part, part, send, line_recv.at[ch, slot], expert)
+
+    def up_copy(ch, d):
+        return line_copy(ch, level - d, up_send.at[ch, d], me + plane)
+
+    def down_copy(ch, d):
+        return line_copy(ch, level + d, down_send.at[ch, d], me - plane)
+
+    def pair_copy(ch, slot):
         return remote(
-            line_own.at[ch, rows_of(0, tok)],
-            line_own.at[ch, rows_of(k, tok)],
-            line_send.at[ch, k - 1],
-            line_recv.at[ch, k - 1],
-            ahead[k],
-        )
-
-    def pair_copy(ch):
-        return remote(line_own.at[ch], line_pair.at[ch], pair_send.at[ch], pair_recv.at[ch], pair_id)
+            line_own.at[ch, rows_of(slot, tok)],
+            line_pair.at[ch, rows_of(slot, tok)],
+            pair_send.at[ch, slot],
+            pair_recv.at[ch, slot],
+            pair_id,
+        )
 
     def leaf_copy(ch, g):
         return remote(
@@ -166,21 +174,16 @@
 
     def end_copy(ch, k):
         return remote(
-            line_sum.at[ch, rows_of(k, tok)],
+            line_sum.at[ch, rows_of(lax.rem(level + slots - k, slots), tok)],
             line_got.at[ch, rows_of(k - 1, tok)],
             end_send.at[ch, k - 1],
             end_recv.at[ch, k - 1],
             behind[k],
         )
 
-    def table_line(k):
-        return remote(
-            table_own.at[rows_of(0, tok)],
-            table_own.at[rows_of(k, tok)],
-            table_send.at[k],
-            table_recv.at[k],
-            ahead[k],
-        )
+    def table_line(k, slot):
+        part = table_own.at[rows_of(slot, tok)]
+        return remote(part, part, table_send.at[k], table_recv.at[k], ahead[k])
 
     def table_across():
         return remote(table_own, table_pair, table_send.at[0], table_recv.at[0], pair_id)
@@ -209,31 +212,42 @@
     for expert, side in ((pair_id, core), (leaf_id, core), (me, 1 - core)):
         pl.semaphore_signal(barrier, inc=1, device_id={"expert": expert, "dp": side}, device_id_type=MESH)
 
-    lanes = lax.broadcasted_iota(jnp.int32, table_pair.shape[:0] + (tok, table_pair.shape[1]), 1)
     raw = weight_ref[...]
-    share = raw / jnp.sum(raw, axis=-1, keepdims=True)
+    share = raw / jnp.sum(raw, axis=0, keepdims=True)
     named = ids_ref[...]
-    entry = jnp.zeros(lanes.shape, jnp.float32)
+    place = lax.broadcasted_iota(jnp.int32, (table_own.shape[1], tok), 0)
+    entry = jnp.zeros(place.shape, jnp.float32)
     for k in range(TOPK):
-        entry = entry + jnp.where(lanes == named[:, k : k + 1], share[:, k : k + 1], 0.0)
-    table_own[pl.ds(0, tok), :] = entry.astype(jnp.bfloat16)
+        entry = entry + jnp.where(place == named[k : k + 1], share[k : k + 1], 0.0)
+    table_own[rows_of(level, tok), :] = entry.T.astype(jnp.bfloat16)
 
     widened = tok_ref[...].astype(jnp.float32)
     inverse = lax.rsqrt(jnp.mean(widened * widened, axis=-1, keepdims=True) + 1e-06)
     for ch in range(chunks):
         cols = pl.ds(ch * span, span)
-        line_own[ch, pl.ds(0, tok), :] = (
+        line_own[ch, rows_of(level, tok), :] = (
             tok_ref[:, cols].astype(jnp.float32) * inverse * gain_ref[:, cols]
         ).astype(jnp.bfloat16)
 
     pl.semaphore_wait(barrier, slots - 1 + 3)
 
     for k in range(1, slots):
-        table_line(k).start()
+        table_line(k, level).start()
+
+    def pass_up(ch, d):
+        @pl.when((level >= d) & (level + 1 < slots))
+        def _():
+            up_copy(ch, d).start()
+
+    def pass_down(ch, d):
+        @pl.when((level + d < slots) & (level >= 1))
+        def _():
+            down_copy(ch, d).start()
 
     def send_line(ch, carry):
-        for k in range(1, slots):
-            line_copy(ch, k).start()
+        pass_up(ch, 0)
+        pass_down(ch, 0)
+        pair_copy(ch, level).start()
         return carry
 
     lax.fori_loop(0, chunks, send_line, 0)
@@ -259,7 +273,7 @@
     my_expert, leaf_expert = holder_ref[me], holder_ref[leaf_id]
 
     for k in range(1, slots):
-        table_line(k).wait_recv()
+        table_line(k, lax.rem(level + slots - k, slots)).wait_recv()
     table_across().start()
     choose(table_own, leaf_expert, 1)
     choose(table_own, my_expert, 0)
@@ -315,18 +329,34 @@
         gate = acc[:, : 2 * unit]
         hid[...] = (gate / (1.0 + jnp.exp(-gate)) * acc[:, 2 * unit :]).astype(jnp.bfloat16)
 
-    def gather(i, carry):
-        @pl.when(i < chunks)
-        def _():
-            for k in range(1, slots):
-                line_copy(i, k).wait_recv()
-            pair_copy(i).start()
-            packed[i, pl.ds(0, room), :] = pick(1, line_own[i])
-            mine_rows[i, pl.ds(0, room), :] = pick(0, line_own[i])
-            leaf_copy(i, 0).start()
-            attend(i)
-
-        @pl.when(i == 1)
+    def hop(ch, d):
+        @pl.when(level >= d)
+        def _():
+            line_copy(ch, level - d, up_send.at[ch, 0], me).wait_recv()
+            pair_copy(ch, level - d).start()
+
+        pass_up(ch, d)
+
+        @pl.when(level + d < slots)
+        def _():
+            line_copy(ch, level + d, up_send.at[ch, 0], me).wait_recv()
+            pair_copy(ch, level + d).start()
+
+        pass_down(ch, d)
+
+    def during(place, work):
+        @pl.when((place >= 0) & (place < chunks))
+        def _():
+            work(place)
+
+    def own_ready(ch):
+        packed[ch, pl.ds(0, room), :] = pick(1, line_own[ch])
+        mine_rows[ch, pl.ds(0, room), :] = pick(0, line_own[ch])
+        leaf_copy(ch, 0).start()
+        attend(ch)
+
+    def pair_ready(ch):
+        @pl.when(ch == 0)
         def _():
             table_across().wait_recv()
             choose(table_pair, leaf_expert, 3)
@@ -335,29 +365,33 @@
                 load(n).wait()
                 give(n).wait_recv()
 
-        @pl.when((i >= 1) & (i <= chunks))
-        def _():
-            j = i - 1
-            pair_copy(j).wait_recv()
-            packed[j, pl.ds(room, room), :] = pick(3, line_pair[j])
-            mine_rows[j, pl.ds(room, room), :] = pick(2, line_pair[j])
-            leaf_copy(j, 1).start()
-            project(mine_acc, mine_rows[j], j)
-
-        @pl.when(i == chunks + 1)
+        for slot in range(slots):
+            pair_copy(ch, slot).wait_recv()
+        packed[ch, pl.ds(room, room), :] = pick(3, line_pair[ch])
+        mine_rows[ch, pl.ds(room, room), :] = pick(2, line_pair[ch])
+        leaf_copy(ch, 1).start()
+        project(mine_acc, mine_rows[ch], ch)
+
+        @pl.when(ch == chunks - 1)
         def _():
             activate(mine_acc, mine_hid)
 
-        @pl.when(i >= 2)
-        def _():
-            j = i - 2
-            for g in range(2):
-                leaf_copy(j, g).wait_recv()
-            project(leaf_acc, leaf_rows[j], j)
-
+    def leaf_ready(ch):
+        for g in range(2):
+            leaf_copy(ch, g).wait_recv()
+        project(leaf_acc, leaf_rows[ch], ch)
+
+    reach = slots - 1
+
+    def gather(i, carry):
+        for d in range(reach, 0, -1):
+            during(i - (d - 1), lambda ch, d=d: hop(ch, d))
+        during(i - (reach - 1), own_ready)
+        during(i - reach, pair_ready)
+        during(i - (reach + 1), leaf_ready)
         return carry
 
-    lax.fori_loop(0, chunks + 2, gather, 0)
+    lax.fori_loop(0, chunks + reach + 1, gather, 0)
     activate(leaf_acc, leaf_hid)
 
     def shrink(hid, ch):
@@ -408,7 +442,7 @@
             j = i - 2
             cols = pl.ds(pl.multiple_of(j * span, span), span)
             total = tok_ref[:, cols].astype(jnp.float32) + context[j]
-            mixture = line_sum[j, pl.ds(0, tok), :].astype(jnp.float32)
+            mixture = line_sum[j, rows_of(level, tok), :].astype(jnp.float32)
             for k in range(1, slots):
                 end_copy(j, k).wait_recv()
                 mixture = mixture + line_got[j, rows_of(k - 1, tok), :].astype(jnp.float32)
@@ -419,20 +453,30 @@
     lax.fori_loop(0, chunks + 2, reduce, 0)
 
     def finish(ch, carry):
+        for d in range(slots - 1):
+
+            @pl.when((level >= d) & (level + 1 < slots))
+            def _(d=d):
+                up_copy(ch, d).wait_send()
+
+            @pl.when((level + d < slots) & (level >= 1))
+            def _(d=d):
+                down_copy(ch, d).wait_send()
+
         for k in range(1, slots):
-            line_copy(ch, k).wait_send()
             end_copy(ch, k).wait_send()
+        for slot in range(slots):
+            pair_copy(ch, slot).wait_send()
         for g in range(2):
             leaf_copy(ch, g).wait_send()
             back_copy(ch, g).wait_send()
-        pair_copy(ch).wait_send()
         sum_copy(ch).wait_send()
         return carry
 
     lax.fori_loop(0, chunks, finish, 0)
     table_across().wait_send()
     for k in range(1, slots):
-        table_line(k).wait_send()
+        table_line(k, level).wait_send()
     for n in range(3):
         give(n).wait_send()
 
@@ -496,8 +540,9 @@
             pltpu.VMEM((4, full, room), bf16),
             dma((chunks, slots - 1)),
             dma((chunks, slots - 1)),
-            dma((chunks,)),
-            dma((chunks,)),
+            dma((chunks, slots)),
+            dma((chunks, slots)),
+            dma((chunks, slots)),
             dma((chunks, 2)),
             dma((chunks, 2)),
             dma((chunks, 2)),
@@ -523,8 +568,8 @@
         prompt_keys,
         prompt_values,
         norm_gain.reshape(1, width),
-        expert_ids,
-        route_weight,
+        expert_ids.T,
+        route_weight.T,
         holder,
         stored_gate,
         stored_up,

time: 157 us -> 144 us (0.917)
  Pallas kernels: 152 us -> 142 us
  local copies, waits for them, and re-layouts: 4.62 us -> 1.87 us
    pallas_call x1, Pallas kernels: 152 us -> 142 us  [fused_layer(): pl.pallas_call(functools.partial(layer_body, slots, chunks, room), out_sh...]
    unnamed x3 -> x1, local copies, waits for them, and re-layouts: 4.62 us -> 1.87 us
where the time goes in v2:
time: 144 us; the launch traced here: 143 us
  Pallas kernels  142 us (99%)
  local copies, waits for them, and re-layouts  1.87 us (1%)
    pallas_call x1, Pallas kernels, fused_layer(): pl.pallas_call(functools.partial(layer_body, slots, chunks, room), out_sh...  142 us

profile of v2, /device:TPU:0, one launch (start us, length us, event | category | flops | bytes accessed | tf_op | source)
XLA Modules:
  0.0 143.4 jit_solution(6033625138055302447)
XLA Ops:
  0.0 141.5 %shard_map.127 = bf16[64,4096]{1,0:T(8,128)(2,1)} custom-call(bf16[64,4096]{1,0:T(8,128)(2,1)} %tok_ref.1, bf16[64,4096]{1,0:T(8,128)(2,1)} %query_ref.1, bf16[64,256]{1,0:T(8,128)(2,1)} %key_ref.1, bf16[64,256]{1,0:T(8,128)(2,1)} %value_ref.1, bf16[1024,256]{1,0:T(8,128)(2,1)} %pkey_ref.1, bf16[1024,256]{1,0:T(8,128)(2,1)} %pvalue_ref.1, ...), custom_call_target="tpu_custom_call" | custom-call | tf_op jit(solution)/shard_map/pallas_call | solution.py:512
  141.5 1.9 %copy.15 = bf16[64,4096]{1,0:T(8,128)(2,1)} copy(bf16[64,4096]{1,0:T(8,128)(2,1)} %shard_map.127) | data formatting | bytes 1048576
